TPU v7x, 128 devices: a whole 4x4x4 slice. The times are simulated.
128 devices in a mesh: grp: 8 (over z_hi, x), ep: 8 (over y, core), tp: 2 (over z_lo).
Axes of the slice: x: 4, y: 4, z: 4 (z_hi: 2, z_lo: 2; z = z_hi * 2 + z_lo), core: 2. Of those that a mesh axis runs over, the one named last changes fastest.
Arguments:
- residual: bfloat16 [2048, 4096], P(('grp', 'ep'), 'tp'), may hold values from -400 to 400
- queries: bfloat16 [2048, 4096], P(('grp', 'ep'), 'tp'), may hold values from -8 to 8
- token_key_value: bfloat16 [2048, 2, 1024], P(('grp', 'ep'), None, 'tp'), may hold values from -4 to 4
- cache: bfloat16 [2048, 2, 192, 1024], P(('grp', 'ep'), None, None, 'tp'), may hold values from -8 to 8
- cache_length: int32 [2048], P(('grp', 'ep')), may hold values from 2 to 192, as said below
- active: int32 [2048], P(('grp', 'ep')), may hold values from 0 to 1, as said below
- routes: int32 [2048, 2], P(('grp', 'ep')), may hold values from 0 to 7, as said below
- norm_gain: bfloat16 [4096], P('tp'), may hold values from 0.099609375 to 1.8984375
- router: bfloat16 [4096, 8], P('tp'), may hold values from -0.09375 to 0.09375
- w_gate: bfloat16 [8, 4096, 8192], P('ep', ('grp', 'tp')), may hold values from -0.09375 to 0.09375
- w_up: bfloat16 [8, 4096, 8192], P('ep', ('grp', 'tp')), may hold values from -0.09375 to 0.09375
- w_down: bfloat16 [8, 4096, 8192], P('ep', ('grp', 'tp')), may hold values from -0.0625 to 0.0625
Outputs:
- delta: bfloat16 [2048, 4096], P(('grp', 'ep'), 'tp')
Inputs may be any that keep to these rules, and one draw needn't show every extreme that they name: `cache_length`: every device's 32 sequences include one with 192 cached positions. The sequences that name their group's common expert first (see routes) all have active = 1. `routes`: each sequence names two different experts; among the sequences of one device no expert is named more than 16 times, and one expert, the same for every device of a grp index, is named first by exactly 16 of each such device's sequences.
All inputs are finite; a program needn't handle non-finite values.
Results may differ from a plain program's by a relative error of at most 0.012.
Values may be sent and summed in bfloat16 or wider, within the bound.
A program may use at most 192 MiB of HBM per device.

v0:
```python
import jax
import jax.numpy as jnp
from jax import lax
from jax.sharding import PartitionSpec as P

MODEL_WIDTH = 4096
QUERY_HEADS = 32
KEY_VALUE_HEADS = 8
HEAD_SIZE = 128
EPSILON = 1e-05


def attend_local(queries, token_key_value, cache, cache_length):
    seq_count = queries.shape[0]
    positions = cache.shape[2]
    heads_kv = cache.shape[3] // HEAD_SIZE
    group_share = QUERY_HEADS // KEY_VALUE_HEADS
    score_scale = HEAD_SIZE ** (-0.5)
    query_head_rows = queries.reshape(seq_count, heads_kv, group_share, HEAD_SIZE)
    stored_keys = cache[:, 0].reshape(seq_count, positions, heads_kv, HEAD_SIZE)
    stored_values = cache[:, 1].reshape(seq_count, positions, heads_kv, HEAD_SIZE)
    incoming_key = token_key_value[:, 0].reshape(seq_count, heads_kv, HEAD_SIZE)
    incoming_value = token_key_value[:, 1].reshape(seq_count, heads_kv, HEAD_SIZE)
    scores = (
        jnp.einsum(
            "skgd,slkd->skgl", query_head_rows, stored_keys, preferred_element_type=jnp.float32
        )
        * score_scale
    )
    in_cache = (
        jnp.arange(positions, dtype=jnp.int32)[None, None, None, :]
        < cache_length[:, None, None, None]
    )
    scores = jnp.where(in_cache, scores, -jnp.inf)
    self_score = (
        jnp.einsum(
            "skgd,skd->skg", query_head_rows, incoming_key, preferred_element_type=jnp.float32
        )
        * score_scale
    )
    highest = jnp.maximum(jnp.max(scores, axis=-1), self_score)
    exponent = jnp.exp(scores - highest[..., None])
    own_exp = jnp.exp(self_score - highest)
    totals = jnp.sum(exponent, axis=-1) + own_exp
    normalized = (exponent / totals[..., None]).astype(jnp.bfloat16)
    own_weight = (own_exp / totals).astype(jnp.bfloat16)
    mixture = jnp.einsum(
        "skgl,slkd->skgd", normalized, stored_values, preferred_element_type=jnp.float32
    )
    mixture = (
        mixture
        + own_weight.astype(jnp.float32)[..., None]
        * incoming_value.astype(jnp.float32)[:, :, None, :]
    )
    return mixture.reshape(seq_count, heads_kv * group_share * HEAD_SIZE).astype(jnp.bfloat16)


def per_device(
    residual,
    queries,
    token_key_value,
    cache,
    cache_length,
    active,
    routes,
    norm_gain,
    router,
    w_gate,
    w_up,
    w_down,
):
    tp_count = lax.axis_size("tp")
    tp_rank = lax.axis_index("tp")
    gate_serve, up_serve = (
        lax.all_to_all(w_gate, ("grp", "tp"), split_axis=2, concat_axis=1, tiled=True),
        lax.all_to_all(w_up, ("grp", "tp"), split_axis=2, concat_axis=1, tiled=True),
    )
    attention_output = attend_local(queries, token_key_value, cache, cache_length)
    state = residual.astype(jnp.float32) + attention_output.astype(jnp.float32)
    scaled = state * norm_gain.astype(jnp.float32)[None, :]
    squares, raw_logits = lax.psum(
        (
            jnp.sum(state * state, axis=1),
            jnp.dot(scaled, router.astype(jnp.float32), precision=lax.Precision.HIGHEST),
        ),
        "tp",
    )
    row_scale = jnp.sqrt(squares / MODEL_WIDTH + EPSILON)[:, None]
    logits = raw_logits / row_scale
    normed = lax.all_gather((scaled / row_scale).astype(jnp.bfloat16), "tp", axis=1, tiled=True)
    chosen = jnp.take_along_axis(logits, routes, axis=1)
    weight_first = jax.nn.sigmoid(chosen[:, 0] - chosen[:, 1])
    weight_second = 1.0 - weight_first
    seq_count = residual.shape[0]
    expert_count = router.shape[1]
    half_cap = seq_count // 2 // tp_count
    slot_total = half_cap * expert_count
    still_live = active == 1
    flat_expert = routes.reshape(-1)
    flat_live = jnp.repeat(still_live, 2)
    onehot = (
        (flat_expert[:, None] == jnp.arange(expert_count, dtype=jnp.int32)[None, :])
        & flat_live[:, None]
    ).astype(jnp.int32)
    before = jnp.cumsum(onehot, axis=0) - onehot
    rank_order = jnp.sum(before * onehot, axis=1)
    owner_half = rank_order // half_cap
    slot_index = rank_order % half_cap * expert_count + flat_expert
    on_this_half = flat_live & (owner_half == tp_rank)
    selector = (
        (
            (slot_index[:, None] == jnp.arange(slot_total, dtype=jnp.int32)[None, :])
            & on_this_half[:, None]
        )
        .astype(jnp.bfloat16)
        .reshape(seq_count, 2, slot_total)
    )
    senders = selector[:, 0] + selector[:, 1]
    outgoing = lax.dot_general(
        senders, normed, (((0,), (0,)), ((), ())), preferred_element_type=jnp.float32
    )
    outgoing = outgoing.astype(jnp.bfloat16).reshape(half_cap, expert_count, normed.shape[1])
    arrived = lax.all_to_all(outgoing, "ep", split_axis=1, concat_axis=0, tiled=True)
    portion = lax.all_gather(arrived, ("grp", "tp"), axis=0, tiled=True)
    gate_part = jnp.einsum("red,edf->ref", portion, gate_serve, preferred_element_type=jnp.float32)
    up_part = jnp.einsum("red,edf->ref", portion, up_serve, preferred_element_type=jnp.float32)
    hidden = (jax.nn.silu(gate_part) * up_part).astype(jnp.bfloat16)
    partial_sums = jnp.einsum(
        "ref,edf->red",
        lax.all_gather(hidden, ("grp", "tp"), axis=2, tiled=True),
        w_down,
        preferred_element_type=jnp.float32,
    )
    results = lax.all_to_all(
        partial_sums.astype(jnp.bfloat16), ("grp", "tp"), split_axis=0, concat_axis=2, tiled=True
    )
    returned = lax.all_to_all(results, "ep", split_axis=0, concat_axis=1, tiled=True).reshape(
        slot_total, normed.shape[1]
    )
    pick_first = jnp.dot(selector[:, 0], returned, preferred_element_type=jnp.float32)
    pick_second = jnp.dot(selector[:, 1], returned, preferred_element_type=jnp.float32)
    combined = weight_first[:, None] * pick_first + weight_second[:, None] * pick_second
    moe_sum = lax.psum_scatter(
        combined.astype(jnp.bfloat16), "tp", scatter_dimension=1, tiled=True
    ).astype(jnp.float32)
    delta = jnp.where(still_live[:, None], attention_output.astype(jnp.float32) + moe_sum, 0.0)
    return delta.astype(jnp.bfloat16)


def solution(mesh):
    in_specs = (
        P(("grp", "ep"), "tp"),
        P(("grp", "ep"), "tp"),
        P(("grp", "ep"), None, "tp"),
        P(("grp", "ep"), None, None, "tp"),
        P(("grp", "ep")),
        P(("grp", "ep")),
        P(("grp", "ep"), None),
        P("tp"),
        P("tp", None),
        P("ep", ("grp", "tp"), None),
        P("ep", ("grp", "tp"), None),
        P("ep", ("grp", "tp"), None),
    )
    out_specs = P(("grp", "ep"), "tp")
    return jax.shard_map(
        per_device, mesh=mesh, in_specs=in_specs, out_specs=out_specs, check_vma=False
    )
```

profile of v0, /device:TPU:1, one launch (start us, length us, event | category | flops | bytes accessed | tf_op | source)
XLA Modules:
  0.0 794.2 jit_solution(5515043613989613150)
XLA Ops:
  6.5 10.5 %fusion.74 = (bf16[32,1,192,512]{3,2,1,0:T(8,128)(2,1)}, bf16[32,1,192,512]{3,2,1,0:T(8,128)(2,1)}) fusion(bf16[32,2,192,512]{3,2,1,0:T(8,128)(2,1)} %param.15), kind=kLoop, calls=%fused_computation.95 | loop fusion | bytes 25165824 | tf_op jit(solution)/shard_map/slice | solution.py:20
  17.1 9.8 %reshape_squeeze.10 = bf16[32,192,4,128]{3,2,1,0:T(4,128)(2,1)} reshape(bf16[32,1,192,512]{3,2,1,0:T(8,128)(2,1)} %get-tuple-element.9) | data formatting | bytes 12582912 | tf_op jit(solution)/shard_map/reshape;squeeze | solution.py:20
  27.4 6.2 fusion.75
  34.2 9.8 %reshape_squeeze.12 = bf16[32,192,4,128]{3,2,1,0:T(4,128)(2,1)} reshape(bf16[32,1,192,512]{3,2,1,0:T(8,128)(2,1)} %get-tuple-element.10) | data formatting | bytes 12582912 | tf_op jit(solution)/shard_map/reshape;squeeze | solution.py:21
  49.1 4.9 all-reduce
  60.5 16.5 %all_to_all.82 = bf16[8,8,4096]{2,0,1:T(8,128)(2,1)} all-to-all(bf16[8,8,4096]{2,0,1:T(8,128)(2,1)S(1)} %copy.90), channel_id=1, replica_groups=mesh['grp'=8,'ep'=8,'tp'=2] {'ep'}, dimensions={1} | all-to-all | bytes 1048576 | tf_op jit(solution)/shard_map/all_to_all | solution.py:123
  77.0 18.0 %copy.91 = bf16[1,256,8192]{1,0,2:T(2,128)(2,1)} copy(bf16[1,256,8192]{2,1,0:T(8,128)(2,1)} %param.21) | data formatting | bytes 8388608 | tf_op args[9]
  95.5 43.5 %reduce.4 = bf16[8192,256]{1,0:T(8,128)(2,1)} reduce(bf16[8192,1,256]{2,1,0:T(2,128)(2,1)} %bitcast.117, bf16[]{:T(256)} %broadcast.143), dimensions={1}, to_apply=%bitcast.106.reduce_sub_computation | reduce | bytes 8388610
  138.9 10.5 %reshape.180 = bf16[16,2,65536]{2,1,0:T(2,128)(2,1)} reshape(bf16[8192,256]{1,0:T(8,128)(2,1)} %reduce.4) | data formatting | bytes 8388608
  149.4 7.7 all-to-all-start.1
  157.1 17.9 %copy.93 = bf16[1,256,8192]{1,0,2:T(2,128)(2,1)} copy(bf16[1,256,8192]{2,1,0:T(8,128)(2,1)} %param.22) | data formatting | bytes 8388608 | tf_op args[10]
  175.0 43.5 %reduce.5 = bf16[8192,256]{1,0:T(8,128)(2,1)} reduce(bf16[8192,1,256]{2,1,0:T(2,128)(2,1)} %bitcast.120, bf16[]{:T(256)} %broadcast.143), dimensions={1}, to_apply=%bitcast.108.reduce_sub_computation | reduce | bytes 8388610
  218.5 10.5 %reshape.182 = bf16[16,2,65536]{2,1,0:T(2,128)(2,1)} reshape(bf16[8192,256]{1,0:T(8,128)(2,1)} %reduce.5) | data formatting | bytes 8388608
  229.0 8.5 %all-to-all-done.1 = bf16[16,2,65536]{2,1,0:T(2,128)(2,1)} async-done(((bf16[16,2,65536]{2,1,0:T(2,128)(2,1)}), bf16[16,2,65536]{2,1,0:T(2,128)(2,1)}, u32[]{:S(2)}, u32[]{:S(2)}) %all-to-all-start.1) | async-done | bytes 4194336 | tf_op jit(solution)/shard_map/all_to_all | solution.py:75
  237.5 10.9 %all-to-all-start.2 = ((bf16[16,2,65536]{2,1,0:T(2,128)(2,1)}), bf16[16,2,65536]{2,1,0:T(2,128)(2,1)}, u32[]{:S(2)}, u32[]{:S(2)}) async-start(bf16[16,2,65536]{2,1,0:T(2,128)(2,1)} %reshape.182), calls=%async_computation.2 | async-start | bytes 8388608 | tf_op jit(solution)/shard_map/all_to_all | solution.py:76
  248.5 12.4 %reshape.181 = bf16[8192,1,256]{2,1,0:T(2,128)(2,1)} reshape(bf16[16,2,65536]{2,1,0:T(2,128)(2,1)} %all-to-all-done.1) | data formatting | bytes 8388608
  260.9 6.1 copy.101
  266.9 6.4 copy.92
  273.3 50.0 %all-to-all-done.2 = bf16[16,2,65536]{2,1,0:T(2,128)(2,1)} async-done(((bf16[16,2,65536]{2,1,0:T(2,128)(2,1)}), bf16[16,2,65536]{2,1,0:T(2,128)(2,1)}, u32[]{:S(2)}, u32[]{:S(2)}) %all-to-all-start.2) | async-done | bytes 4194336 | tf_op jit(solution)/shard_map/all_to_all | solution.py:76
  323.3 12.4 %reshape.183 = bf16[8192,1,256]{2,1,0:T(2,128)(2,1)} reshape(bf16[16,2,65536]{2,1,0:T(2,128)(2,1)} %all-to-all-done.2) | data formatting | bytes 8388608
  335.7 6.1 copy.102
  341.8 6.4 copy.94
  348.2 5.4 all-gather.3.cloned.1.call-done
  353.7 8.5 %fusion.4 = f32[1024,512]{1,0:T(8,128)S(1)} fusion(bf16[4096,512]{1,0:T(8,128)(2,1)} %bitcast.125, bf16[1024,1,4096]{2,0,1:T(8,128)(2,1)} %all-gather.3.cloned.1.call-done), kind=kOutput, calls=%fused_computation.5 | convolution fusion | flops 4294967296 | bytes 14680064 | tf_op jit(solution)/shard_map/red,edf->ref/dot_general | solution.py:125
  362.2 5.7 fusion.14
  367.9 347.5 %all-gather.5.cloned.1.call-done = bf16[1024,1,8192]{2,0,1:T(8,128)(2,1)} async-done(((bf16[1024,1,512]{2,0,1:T(8,128)(2,1)}), bf16[1024,1,8192]{2,0,1:T(8,128)(2,1)}) %all-gather.5.cloned.1.call-update) | async-done | bytes 16777232 | tf_op jit(solution)/shard_map/all_gather | solution.py:130
  715.5 11.5 %fusion.25 = bf16[1024,1,256]{2,0,1:T(8,128)(2,1)S(1)} fusion(bf16[1,256,8192]{2,1,0:T(8,128)(2,1)} %param.23, bf16[1024,1,8192]{2,0,1:T(8,128)(2,1)} %all-gather.5.cloned.1.call-done), kind=kOutput, calls=%fused_computation.26 | convolution fusion | flops 4295229440 | bytes 21495808 | tf_op jit(solution)/shard_map/ref,edf->red/dot_general | solution.py:128
  728.9 11.3 %all-to-all-start.3 = ((bf16[16,2,8192]{2,1,0:T(2,128)(2,1)}), bf16[16,2,8192]{2,1,0:T(2,128)(2,1)S(1)}, u32[]{:S(2)}, u32[]{:S(2)}) async-start(bf16[16,2,8192]{2,1,0:T(2,128)(2,1)} %reshape.184), calls=%async_computation.3 | async-start | bytes 1048576 | tf_op jit(solution)/shard_map/all_to_all | solution.py:134
  740.8 10.2 %all-to-all-done.3 = bf16[16,2,8192]{2,1,0:T(2,128)(2,1)S(1)} async-done(((bf16[16,2,8192]{2,1,0:T(2,128)(2,1)}), bf16[16,2,8192]{2,1,0:T(2,128)(2,1)S(1)}, u32[]{:S(2)}, u32[]{:S(2)}) %all-to-all-start.3) | async-done | bytes 524320 | tf_op jit(solution)/shard_map/all_to_all | solution.py:134
  757.4 6.0 all-to-all-start.4
  764.5 8.3 %all-to-all-done.4 = bf16[8,2,16384]{2,1,0:T(2,128)(2,1)S(1)} async-done(((bf16[8,2,16384]{2,1,0:T(2,128)(2,1)}), bf16[8,2,16384]{2,1,0:T(2,128)(2,1)S(1)}, u32[]{:S(2)}, u32[]{:S(2)}) %all-to-all-start.4) | async-done | bytes 524320 | tf_op jit(solution)/shard_map/all_to_all | solution.py:137
  775.5 10.6 %reduce-scatter.2.cloned.1.call-done = bf16[32,2048]{1,0:T(8,128)(2,1)} async-done(((bf16[32,4096]{1,0:T(8,128)(2,1)}), bf16[32,2048]{1,0:T(8,128)(2,1)}) %reduce-scatter.2.cloned.1.call-update) | async-done | bytes 131088 | tf_op jit(solution)/shard_map/reduce_scatter | solution.py:143
  (87 shorter events, 27.4 us)
Async XLA Ops:
  6.5 42.4 %copy-start = (bf16[2048,8]{0,1:T(8,128)(2,1)S(1)}, bf16[2048,8]{0,1:T(8,128)(2,1)}, u32[]{:S(2)}) copy-start(bf16[2048,8]{0,1:T(8,128)(2,1)} %param.20) | copy-start | bytes 98308
  6.5 347.1 %all-gather.3.cloned.1.call-start = ((), (), s32[]{:S(2)}) async-start(), calls=%async_computation.6 | async-start | bytes 8912896 | tf_op jit(solution)/shard_map/all_gather | solution.py:124
  17.1 9.8 %copy-start.4 = (bf16[32,2048]{1,0:T(8,128)(2,1)S(1)}, bf16[32,2048]{1,0:T(8,128)(2,1)}, u32[]{:S(2)}) copy-start(bf16[32,2048]{1,0:T(8,128)(2,1)} %param.13) | copy-start | bytes 393220
  17.1 9.9 %copy-start.8 = (s32[32]{0:T(128)S(1)}, s32[32]{0:T(128)}, u32[]{:S(2)}) copy-start(s32[32]{0:T(128)} %param.16) | copy-start | bytes 388
  17.1 10.0 %copy-start.5 = (bf16[32,2,512]{2,1,0:T(2,128)(2,1)S(1)}, bf16[32,2,512]{2,1,0:T(2,128)(2,1)}, u32[]{:S(2)}) copy-start(bf16[32,2,512]{2,1,0:T(2,128)(2,1)} %param.14) | copy-start | bytes 196612
  44.0 4.8 copy-start.6
  44.0 4.8 copy-start.3
  44.0 10.0 %copy-start.7 = (s32[32,2]{0,1:T(2,128)S(1)}, s32[32,2]{0,1:T(2,128)}, u32[]{:S(2)}) copy-start(s32[32,2]{0,1:T(2,128)} %param.18) | copy-start | bytes 772
  44.0 10.2 %copy-start.10 = (s32[32]{0:T(128)S(1)}, s32[32]{0:T(128)}, u32[]{:S(2)}) copy-start(s32[32]{0:T(128)} %param.17) | copy-start | bytes 388
  149.4 88.1 %all-to-all-start.1 = ((bf16[16,2,65536]{2,1,0:T(2,128)(2,1)}), bf16[16,2,65536]{2,1,0:T(2,128)(2,1)}, u32[]{:S(2)}, u32[]{:S(2)}) async-start(bf16[16,2,65536]{2,1,0:T(2,128)(2,1)} %reshape.180), calls=%async_computation.1 | async-start | bytes 8388608 | tf_op jit(solution)/shard_map/all_to_all | solution.py:75
  237.5 85.8 %all-to-all-start.2 = ((bf16[16,2,65536]{2,1,0:T(2,128)(2,1)}), bf16[16,2,65536]{2,1,0:T(2,128)(2,1)}, u32[]{:S(2)}, u32[]{:S(2)}) async-start(bf16[16,2,65536]{2,1,0:T(2,128)(2,1)} %reshape.182), calls=%async_computation.2 | async-start | bytes 8388608 | tf_op jit(solution)/shard_map/all_to_all | solution.py:76
  248.4 467.1 %all-gather.5.cloned.1.call-start = ((), (), s32[]{:S(2)}) async-start(), calls=%async_computation.7 | async-start | bytes 17825792 | tf_op jit(solution)/shard_map/all_gather | solution.py:130
  353.7 8.5 %copy-start.2 = (bf16[1,16,256,512]{3,2,1,0:T(8,128)(2,1)S(1)}, bf16[1,16,256,512]{3,2,1,0:T(8,128)(2,1)}, u32[]{:S(2)}) copy-start(bf16[1,16,256,512]{3,2,1,0:T(8,128)(2,1)} %copy.94) | copy-start | bytes 12582916
  353.7 8.5 %copy-start.9 = (bf16[1024,1,4096]{2,0,1:T(8,128)(2,1)S(1)}, bf16[1024,1,4096]{2,0,1:T(8,128)(2,1)}, u32[]{:S(2)}) copy-start(bf16[1024,1,4096]{2,0,1:T(8,128)(2,1)} %all-gather.3.cloned.1.call-done) | copy-start | bytes 25165828
  728.9 22.0 %all-to-all-start.3 = ((bf16[16,2,8192]{2,1,0:T(2,128)(2,1)}), bf16[16,2,8192]{2,1,0:T(2,128)(2,1)S(1)}, u32[]{:S(2)}, u32[]{:S(2)}) async-start(bf16[16,2,8192]{2,1,0:T(2,128)(2,1)} %reshape.184), calls=%async_computation.3 | async-start | bytes 1048576 | tf_op jit(solution)/shard_map/all_to_all | solution.py:134
  757.4 15.4 %all-to-all-start.4 = ((bf16[8,2,16384]{2,1,0:T(2,128)(2,1)}), bf16[8,2,16384]{2,1,0:T(2,128)(2,1)S(1)}, u32[]{:S(2)}, u32[]{:S(2)}) async-start(bf16[8,2,16384]{2,1,0:T(2,128)(2,1)} %reshape.186), calls=%async_computation.4 | async-start | bytes 1048576 | tf_op jit(solution)/shard_map/all_to_all | solution.py:137
  763.4 22.6 %reduce-scatter.2.cloned.1.call-start = ((), (), s32[]{:S(2)}) async-start(), calls=%async_computation.8 | async-start | bytes 393216 | tf_op jit(solution)/shard_map/reduce_scatter | solution.py:143
  763.4 24.3 %copy-start.1 = (bf16[2048,8]{0,1:T(8,128)(2,1)S(1)}, bf16[2048,8]{0,1:T(8,128)(2,1)}, u32[]{:S(2)}) copy-start(bf16[2048,8]{0,1:T(8,128)(2,1)} %param.20) | copy-start | bytes 98308
Sparse Core Ops, SparseCore 0:
  77.1 276.5 all-gather.2
  368.1 347.3 all-gather.4
  775.6 10.3 reduce-scatter.1
where the time goes:
time: 797 us; the launch traced here: 794 us
  waiting for transfers between devices  441 us (55%)
  local copies, waits for them, and re-layouts  144 us (18%)
  other arithmetic  95.3 us (12%)
  matrix products  39 us (5%)
  starting transfers between devices  36 us (5%)
  blocking collectives  25.8 us (3%)
  between operations  13.4 us (2%)
    all_gather x1, waiting for transfers between devices, per_device(): lax.all_gather(hidden, ('grp', 'tp'), axis=2, tiled=True)  348 us
    unnamed x38, local copies, waits for them, and re-layouts  98.4 us
    unnamed x2, other arithmetic  86.9 us
    all_to_all x1, waiting for transfers between devices, per_device(): lax.all_to_all(w_up, ('grp', 'tp'), split_axis=2, concat_axis=1, tiled=True)  50 us
    all_to_all x1, blocking collectives, per_device(): lax.all_to_all(outgoing, 'ep', split_axis=1, concat_axis=0, tiled=True)  16.5 us
  transfers between devices with their start and end apart: 7, of which 7 were waited for; matrix products, arithmetic and copies ran while one was open for 25% of the time, Pallas kernels for 0%

commit v1 on v0

--- a/solution.py
+++ b/solution.py
@@ -127,7 +127,10 @@
     hidden = (jax.nn.silu(gate_part) * up_part).astype(jnp.bfloat16)
     partial_sums = jnp.einsum(
         "ref,edf->red",
-        lax.all_gather(hidden, ("grp", "tp"), axis=2, tiled=True),
+        jnp.concatenate(
+            lax.all_to_all(jnp.stack([hidden] * lax.axis_size(("grp", "tp"))), ("grp", "tp"), 0, 0),
+            axis=2,
+        ),
         w_down,
         preferred_element_type=jnp.float32,
     )

time: 797 us -> 638 us (0.80)
  waiting for transfers between devices: 441 us -> 92.8 us
  blocking collectives: 25.8 us -> 217 us
    all_gather x1 -> x0, waiting for transfers between devices: 348 us -> none  [per_device(): lax.all_gather(hidden, ('grp', 'tp'), axis=2, tiled=True)]
    all_to_all x0 -> x1, blocking collectives: none -> 191 us  [per_device(): lax.all_to_all(jnp.stack([hidden] * lax.axis_size(('grp', 'tp'))), ('grp'...]
    unnamed x38 -> x28, local copies, waits for them, and re-layouts: 98.4 us -> 99 us
  transfers between devices with their start and end apart: 7 -> 6, of which waited for: 7 -> 6; matrix products, arithmetic and copies ran while one was open for 25% -> 31% of each run, Pallas kernels for 0% -> 0%
where the time goes in v1:
time: 638 us; the launch traced here: 635 us
  blocking collectives  217 us (34%)
  local copies, waits for them, and re-layouts  148 us (23%)
  other arithmetic  98.8 us (15%)
  waiting for transfers between devices  92.8 us (15%)
  matrix products  33.9 us (5%)
  starting transfers between devices  30.1 us (5%)
  between operations  13.7 us (2%)
    all_to_all x1, blocking collectives, per_device(): lax.all_to_all(jnp.stack([hidden] * lax.axis_size(('grp', 'tp'))), ('grp'...  191 us
    unnamed x28, local copies, waits for them, and re-layouts  99 us
    unnamed x2, other arithmetic  86.9 us
    all_to_all x1, waiting for transfers between devices, per_device(): lax.all_to_all(w_up, ('grp', 'tp'), split_axis=2, concat_axis=1, tiled=True)  49.6 us
    all_to_all x1, blocking collectives, per_device(): lax.all_to_all(outgoing, 'ep', split_axis=1, concat_axis=0, tiled=True)  16.5 us
  transfers between devices with their start and end apart: 6, of which 6 were waited for; matrix products, arithmetic and copies ran while one was open for 31% of the time, Pallas kernels for 0%

profile of v1, /device:TPU:1, one launch (start us, length us, event | category | flops | bytes accessed | tf_op | source)
XLA Modules:
  0.0 634.9 jit_solution(2411806057443314665)
XLA Ops:
  14.2 10.5 %fusion.72 = (bf16[32,1,192,512]{3,2,1,0:T(8,128)(2,1)}, bf16[32,1,192,512]{3,2,1,0:T(8,128)(2,1)}) fusion(bf16[32,2,192,512]{3,2,1,0:T(8,128)(2,1)} %param.15), kind=kLoop, calls=%fused_computation.95 | loop fusion | bytes 25165824 | tf_op jit(solution)/shard_map/slice | solution.py:20
  24.7 9.7 %reshape_squeeze.10 = bf16[32,192,4,128]{3,2,1,0:T(4,128)(2,1)} reshape(bf16[32,1,192,512]{3,2,1,0:T(8,128)(2,1)} %get-tuple-element.9) | data formatting | bytes 12582912 | tf_op jit(solution)/shard_map/reshape;squeeze | solution.py:20
  34.4 6.2 fusion.73
  41.2 9.8 %reshape_squeeze.12 = bf16[32,192,4,128]{3,2,1,0:T(4,128)(2,1)} reshape(bf16[32,1,192,512]{3,2,1,0:T(8,128)(2,1)} %get-tuple-element.10) | data formatting | bytes 12582912 | tf_op jit(solution)/shard_map/reshape;squeeze | solution.py:21
  56.1 4.9 all-reduce
  66.3 16.5 %all_to_all.87 = bf16[8,8,4096]{2,0,1:T(8,128)(2,1)} all-to-all(bf16[8,8,4096]{2,0,1:T(8,128)(2,1)S(1)} %copy.94), channel_id=1, replica_groups=mesh['grp'=8,'ep'=8,'tp'=2] {'ep'}, dimensions={1} | all-to-all | bytes 1048576 | tf_op jit(solution)/shard_map/all_to_all | solution.py:123
  82.8 18.0 %copy.95 = bf16[1,256,8192]{1,0,2:T(2,128)(2,1)} copy(bf16[1,256,8192]{2,1,0:T(8,128)(2,1)} %param.21) | data formatting | bytes 8388608 | tf_op args[9]
  101.3 43.5 %reduce.5 = bf16[8192,256]{1,0:T(8,128)(2,1)} reduce(bf16[8192,1,256]{2,1,0:T(2,128)(2,1)} %bitcast.124, bf16[]{:T(256)} %broadcast.146), dimensions={1}, to_apply=%bitcast.114.reduce_sub_computation | reduce | bytes 8388610
  144.7 10.5 %reshape.191 = bf16[16,2,65536]{2,1,0:T(2,128)(2,1)} reshape(bf16[8192,256]{1,0:T(8,128)(2,1)} %reduce.5) | data formatting | bytes 8388608
  155.2 7.7 %all-to-all-start.1 = ((bf16[16,2,65536]{2,1,0:T(2,128)(2,1)}), bf16[16,2,65536]{2,1,0:T(2,128)(2,1)}, u32[]{:S(2)}, u32[]{:S(2)}) async-start(bf16[16,2,65536]{2,1,0:T(2,128)(2,1)} %reshape.191), calls=%async_computation.1 | async-start | bytes 8388608 | tf_op jit(solution)/shard_map/all_to_all | solution.py:75
  162.9 17.9 %copy.97 = bf16[1,256,8192]{1,0,2:T(2,128)(2,1)} copy(bf16[1,256,8192]{2,1,0:T(8,128)(2,1)} %param.22) | data formatting | bytes 8388608 | tf_op args[10]
  180.9 43.5 %reduce.4 = bf16[8192,256]{1,0:T(8,128)(2,1)} reduce(bf16[8192,1,256]{2,1,0:T(2,128)(2,1)} %bitcast.127, bf16[]{:T(256)} %broadcast.146), dimensions={1}, to_apply=%bitcast.112.reduce_sub_computation | reduce | bytes 8388610
  224.3 10.5 %reshape.189 = bf16[16,2,65536]{2,1,0:T(2,128)(2,1)} reshape(bf16[8192,256]{1,0:T(8,128)(2,1)} %reduce.4) | data formatting | bytes 8388608
  234.8 8.6 %all-to-all-done.1 = bf16[16,2,65536]{2,1,0:T(2,128)(2,1)} async-done(((bf16[16,2,65536]{2,1,0:T(2,128)(2,1)}), bf16[16,2,65536]{2,1,0:T(2,128)(2,1)}, u32[]{:S(2)}, u32[]{:S(2)}) %all-to-all-start.1) | async-done | bytes 4194336 | tf_op jit(solution)/shard_map/all_to_all | solution.py:75
  243.4 10.9 %all-to-all-start.2 = ((bf16[16,2,65536]{2,1,0:T(2,128)(2,1)}), bf16[16,2,65536]{2,1,0:T(2,128)(2,1)}, u32[]{:S(2)}, u32[]{:S(2)}) async-start(bf16[16,2,65536]{2,1,0:T(2,128)(2,1)} %reshape.189), calls=%async_computation.2 | async-start | bytes 8388608 | tf_op jit(solution)/shard_map/all_to_all | solution.py:76
  254.2 12.4 %reshape.192 = bf16[8192,1,256]{2,1,0:T(2,128)(2,1)} reshape(bf16[16,2,65536]{2,1,0:T(2,128)(2,1)} %all-to-all-done.1) | data formatting | bytes 8388608
  266.6 6.1 copy.107
  272.7 6.4 %copy.96 = bf16[1,16,256,512]{3,2,1,0:T(8,128)(2,1)} copy(bf16[1,16,256,512]{2,3,1,0:T(8,128)(2,1)} %bitcast.128) | data formatting | bytes 8388608 | tf_op jit(solution)/shard_map/all_to_all | solution.py:75
  279.1 49.6 %all-to-all-done.2 = bf16[16,2,65536]{2,1,0:T(2,128)(2,1)} async-done(((bf16[16,2,65536]{2,1,0:T(2,128)(2,1)}), bf16[16,2,65536]{2,1,0:T(2,128)(2,1)}, u32[]{:S(2)}, u32[]{:S(2)}) %all-to-all-start.2) | async-done | bytes 4194336 | tf_op jit(solution)/shard_map/all_to_all | solution.py:76
  328.7 12.4 %reshape.190 = bf16[8192,1,256]{2,1,0:T(2,128)(2,1)} reshape(bf16[16,2,65536]{2,1,0:T(2,128)(2,1)} %all-to-all-done.2) | data formatting | bytes 8388608
  341.1 6.1 copy.108
  347.2 6.4 %copy.98 = bf16[1,16,256,512]{3,2,1,0:T(8,128)(2,1)} copy(bf16[1,16,256,512]{2,3,1,0:T(8,128)(2,1)} %bitcast.129) | data formatting | bytes 8388608 | tf_op jit(solution)/shard_map/all_to_all | solution.py:76
  353.6 6.1 all-gather.2.cloned.1.call-done
  359.7 8.3 %fusion.2 = f32[1024,512]{1,0:T(8,128)S(1)} fusion(bf16[4096,512]{1,0:T(8,128)(2,1)} %bitcast.133, bf16[1024,1,4096]{2,0,1:T(8,128)(2,1)} %all-gather.2.cloned.1.call-done), kind=kOutput, calls=%fused_computation.3 | convolution fusion | flops 4294967296 | bytes 14680064 | tf_op jit(solution)/shard_map/red,edf->ref/dot_general | solution.py:125
  368.0 4.7 fusion.19
  375.4 191.4 %all_to_all.88 = bf16[16,1024,1,512]{1,3,2,0:T(8,128)(2,1)S(1)} all-to-all(bf16[16,1024,1,512]{1,3,2,0:T(8,128)(2,1)S(1)} %stack.2), channel_id=1, replica_groups=mesh['grp'=8,'ep'=8,'tp'=2] {'grp','tp'}, dimensions={0} | all-to-all | bytes 33554432 | tf_op jit(solution)/shard_map/all_to_all | solution.py:131
  566.8 6.9 %fusion.25 = bf16[1024,1,256]{2,0,1:T(8,128)(2,1)S(1)} fusion(bf16[1024,8192]{0,1:T(8,128)(2,1)S(1)} %bitcast.130, bf16[1,256,8192]{2,1,0:T(8,128)(2,1)} %param.23), kind=kOutput, calls=%fused_computation.26 | convolution fusion | flops 4295229440 | bytes 21495808 | tf_op jit(solution)/shard_map/ref,edf->red/dot_general | solution.py:128
  575.6 5.1 all-to-all-start.4
  581.2 9.6 %all-to-all-done.4 = bf16[16,2,8192]{2,1,0:T(2,128)(2,1)S(1)} async-done(((bf16[16,2,8192]{2,1,0:T(2,128)(2,1)}), bf16[16,2,8192]{2,1,0:T(2,128)(2,1)S(1)}, u32[]{:S(2)}, u32[]{:S(2)}) %all-to-all-start.4) | async-done | bytes 524320 | tf_op jit(solution)/shard_map/all_to_all | solution.py:137
  597.3 6.5 %all-to-all-start.5 = ((bf16[8,2,16384]{2,1,0:T(2,128)(2,1)}), bf16[8,2,16384]{2,1,0:T(2,128)(2,1)S(1)}, u32[]{:S(2)}, u32[]{:S(2)}) async-start(bf16[8,2,16384]{2,1,0:T(2,128)(2,1)} %reshape.195), calls=%async_computation.5 | async-start | bytes 1048576 | tf_op jit(solution)/shard_map/all_to_all | solution.py:140
  604.9 8.3 %all-to-all-done.5 = bf16[8,2,16384]{2,1,0:T(2,128)(2,1)S(1)} async-done(((bf16[8,2,16384]{2,1,0:T(2,128)(2,1)}), bf16[8,2,16384]{2,1,0:T(2,128)(2,1)S(1)}, u32[]{:S(2)}, u32[]{:S(2)}) %all-to-all-start.5) | async-done | bytes 524320 | tf_op jit(solution)/shard_map/all_to_all | solution.py:140
  615.9 10.6 %reduce-scatter.2.cloned.1.call-done = bf16[32,2048]{1,0:T(8,128)(2,1)} async-done(((bf16[32,4096]{1,0:T(8,128)(2,1)}), bf16[32,2048]{1,0:T(8,128)(2,1)}) %reduce-scatter.2.cloned.1.call-update) | async-done | bytes 131088 | tf_op jit(solution)/shard_map/reduce_scatter | solution.py:146
  (77 shorter events, 36.0 us)
Async XLA Ops:
  6.5 49.4 %copy-start = (bf16[2048,8]{0,1:T(8,128)(2,1)S(1)}, bf16[2048,8]{0,1:T(8,128)(2,1)}, u32[]{:S(2)}) copy-start(bf16[2048,8]{0,1:T(8,128)(2,1)} %param.20) | copy-start | bytes 98308
  6.5 353.1 %all-gather.2.cloned.1.call-start = ((), (), s32[]{:S(2)}) async-start(), calls=%async_computation.7 | async-start | bytes 8912896 | tf_op jit(solution)/shard_map/all_gather | solution.py:124
  51.0 4.8 copy-start.3
  155.2 88.1 %all-to-all-start.1 = ((bf16[16,2,65536]{2,1,0:T(2,128)(2,1)}), bf16[16,2,65536]{2,1,0:T(2,128)(2,1)}, u32[]{:S(2)}, u32[]{:S(2)}) async-start(bf16[16,2,65536]{2,1,0:T(2,128)(2,1)} %reshape.191), calls=%async_computation.1 | async-start | bytes 8388608 | tf_op jit(solution)/shard_map/all_to_all | solution.py:75
  243.4 85.3 %all-to-all-start.2 = ((bf16[16,2,65536]{2,1,0:T(2,128)(2,1)}), bf16[16,2,65536]{2,1,0:T(2,128)(2,1)}, u32[]{:S(2)}, u32[]{:S(2)}) async-start(bf16[16,2,65536]{2,1,0:T(2,128)(2,1)} %reshape.189), calls=%async_computation.2 | async-start | bytes 8388608 | tf_op jit(solution)/shard_map/all_to_all | solution.py:76
  359.7 8.3 %copy-start.2 = (bf16[1,16,256,512]{3,2,1,0:T(8,128)(2,1)S(1)}, bf16[1,16,256,512]{3,2,1,0:T(8,128)(2,1)}, u32[]{:S(2)}) copy-start(bf16[1,16,256,512]{3,2,1,0:T(8,128)(2,1)} %copy.98) | copy-start | bytes 12582916
  359.7 8.3 %copy-start.5 = (bf16[1024,1,4096]{2,0,1:T(8,128)(2,1)S(1)}, bf16[1024,1,4096]{2,0,1:T(8,128)(2,1)}, u32[]{:S(2)}) copy-start(bf16[1024,1,4096]{2,0,1:T(8,128)(2,1)} %all-gather.2.cloned.1.call-done) | copy-start | bytes 25165828
  566.8 13.9 %copy-start.4 = (s32[32,2]{0,1:T(2,128)S(1)}, s32[32,2]{0,1:T(2,128)}, u32[]{:S(2)}) copy-start(s32[32,2]{0,1:T(2,128)} %param.18) | copy-start | bytes 772
  575.6 15.2 %all-to-all-start.4 = ((bf16[16,2,8192]{2,1,0:T(2,128)(2,1)}), bf16[16,2,8192]{2,1,0:T(2,128)(2,1)S(1)}, u32[]{:S(2)}, u32[]{:S(2)}) async-start(bf16[16,2,8192]{2,1,0:T(2,128)(2,1)} %reshape.193), calls=%async_computation.4 | async-start | bytes 1048576 | tf_op jit(solution)/shard_map/all_to_all | solution.py:137
  597.3 15.9 %all-to-all-start.5 = ((bf16[8,2,16384]{2,1,0:T(2,128)(2,1)}), bf16[8,2,16384]{2,1,0:T(2,128)(2,1)S(1)}, u32[]{:S(2)}, u32[]{:S(2)}) async-start(bf16[8,2,16384]{2,1,0:T(2,128)(2,1)} %reshape.195), calls=%async_computation.5 | async-start | bytes 1048576 | tf_op jit(solution)/shard_map/all_to_all | solution.py:140
  603.8 22.6 %reduce-scatter.2.cloned.1.call-start = ((), (), s32[]{:S(2)}) async-start(), calls=%async_computation.8 | async-start | bytes 393216 | tf_op jit(solution)/shard_map/reduce_scatter | solution.py:146
  603.8 24.3 %copy-start.1 = (bf16[2048,8]{0,1:T(8,128)(2,1)S(1)}, bf16[2048,8]{0,1:T(8,128)(2,1)}, u32[]{:S(2)}) copy-start(bf16[2048,8]{0,1:T(8,128)(2,1)} %param.20) | copy-start | bytes 98308
Sparse Core Ops, SparseCore 0:
  82.9 276.7 all-gather.1
  616.0 10.3 reduce-scatter.1
